TPU v7x, 32 devices: a whole 2x2x4 slice. The times are simulated.
32 devices in a mesh: dp: 8 (over z, y), tensor: 4 (over x, core).
Axes of the slice: x: 2, y: 2, z: 4, core: 2. Of those that a mesh axis runs over, the one named last changes fastest.
Arguments:
- query: bfloat16 [64, 64, 128], P('dp', 'tensor'), may hold values from -8 to 8
- kv_pages: bfloat16 [560, 8, 2, 128, 128], P('dp', 'tensor'), may hold values from -8 to 8
- move_plan: int32 [8, 3, 12], P('dp'), may hold values from 0 to 69, as said below
- move_count: int32 [8], P('dp'), may hold values from 9 to 12
- block_table: int32 [64, 8], P('dp'), may hold values from 0 to 69, as said below
- seq_lens: int32 [64], P('dp'), may hold values from 1 to 1024
- out_weight: bfloat16 [8192, 8192], P('tensor', 'dp'), may hold values from -0.0625 to 0.0625
Outputs:
- new_pages: bfloat16 [560, 8, 2, 128, 128], P('dp', 'tensor')
- projected: bfloat16 [64, 8192], P(None, 'dp')
Inputs may be any that keep to these rules, and one draw needn't show every extreme that they name: `move_plan`: row 0 holds the device's own source slots, distinct within a device; row 1 target devices; row 2 target slots. Entries at or past the device's move_count are padding to be ignored. At most 2 valid moves go from one device to one device, and some pair has exactly 2. The (target device, target slot) pairs of all valid moves are distinct. `block_table`: all entries of the sequences of one device are distinct slots of that device; sequence s belongs to device s // 8.
All inputs are finite; a program needn't handle non-finite values.
Results may differ from a plain program's by a relative error of at most 0.0055.
Values may be sent and summed in bfloat16 or wider, within the bound.
No kernel may reach another device: no remote copies, remote signals or barrier semaphores. Data moves between devices by JAX's collectives and lax.ppermute only.
A program may use at most 128 MiB of HBM per device.

v0:
```python
import math
import jax
import jax.numpy as jnp
from jax import lax
from jax.sharding import PartitionSpec as P

HD = 128
BLOCK = 128
BLOCKS = 8
CAP = 2


def body(query, kv_pages, move_plan, move_count, block_table, seq_lens, out_weight):
    slots_here = kv_pages.shape[0]
    move_total = move_plan.shape[2]
    devices = lax.axis_size("dp")
    capacity = CAP
    holding_rows = devices * capacity
    move_list = move_plan[0]
    move_index = jnp.arange(move_total, dtype=jnp.int32)
    is_valid = move_index < move_count[0]
    target_dev = move_list[1]
    earlier = (
        (target_dev[:, None] == target_dev[None, :])
        & is_valid[None, :]
        & (move_index[None, :] < move_index[:, None])
    )
    dest_rank = jnp.sum(earlier.astype(jnp.int32), axis=1)
    send_row = jnp.where(is_valid, target_dev * capacity + dest_rank, -1)
    flat_pages = kv_pages.reshape(slots_here, -1)
    picked = flat_pages[move_list[0]]
    select = jnp.arange(holding_rows, dtype=jnp.int32)[:, None] == send_row[None, :]
    outgoing = jnp.dot(
        select.astype(jnp.bfloat16), picked, preferred_element_type=jnp.float32
    ).astype(jnp.bfloat16)
    outgoing = outgoing.reshape((holding_rows,) + kv_pages.shape[1:])
    out_slots = jnp.sum(select.astype(jnp.int32) * (move_list[2][None, :] + 1), axis=1) - 1
    slot_tags = out_slots.astype(jnp.float32).astype(jnp.bfloat16)
    arrived, arrived_tags = (
        lax.all_to_all(outgoing, "dp", split_axis=0, concat_axis=0, tiled=True),
        lax.all_to_all(slot_tags, "dp", split_axis=0, concat_axis=0, tiled=True),
    )
    incoming = arrived_tags.astype(jnp.float32).astype(jnp.int32)
    hit_table = jnp.arange(slots_here, dtype=jnp.int32)[:, None] == incoming[None, :]
    placed = jnp.dot(
        hit_table.astype(jnp.bfloat16),
        arrived.reshape(holding_rows, -1),
        preferred_element_type=jnp.float32,
    ).astype(jnp.bfloat16)
    written = jnp.any(hit_table, axis=1)
    new_pages = jnp.where(written[:, None], placed, flat_pages).reshape(kv_pages.shape)
    seq_here = query.shape[0]
    local_heads = new_pages.shape[1]
    head_dim = query.shape[2]
    group_size = query.shape[1] // local_heads
    context = BLOCKS * BLOCK
    gathered = new_pages[block_table]
    key_rows = jnp.transpose(gathered[:, :, :, 0], (0, 2, 1, 3, 4)).reshape(
        seq_here, local_heads, context, head_dim
    )
    value_rows = jnp.transpose(gathered[:, :, :, 1], (0, 2, 1, 3, 4)).reshape(
        seq_here, local_heads, context, head_dim
    )
    grouped = query.reshape(seq_here, local_heads, group_size, head_dim)
    score_scale = 1.0 / math.sqrt(HD)
    scores = (
        jnp.einsum("skgd,sktd->skgt", grouped, key_rows, preferred_element_type=jnp.float32)
        * score_scale
    )
    position = jnp.arange(context, dtype=jnp.int32)
    scores = jnp.where(position[None, None, None, :] < seq_lens[:, None, None, None], scores, -1e30)
    largest = jnp.max(scores, axis=-1, keepdims=True)
    expo = jnp.exp(scores - largest)
    weights = (expo / jnp.sum(expo, axis=-1, keepdims=True)).astype(jnp.bfloat16)
    mixed_heads = jnp.einsum(
        "skgt,sktd->skgd", weights, value_rows, preferred_element_type=jnp.float32
    )
    attention = mixed_heads.reshape(seq_here, local_heads * group_size * head_dim).astype(
        jnp.bfloat16
    )
    partial_sums = jnp.dot(
        lax.all_gather(attention, "dp", axis=0, tiled=True),
        out_weight,
        preferred_element_type=jnp.float32,
    )
    summed = lax.psum(partial_sums, "tensor")
    return (new_pages, summed.astype(jnp.bfloat16))


def solution(mesh):
    placed = (
        P("dp", "tensor", None),
        P("dp", "tensor", None, None, None),
        P("dp", None, None),
        P("dp"),
        P("dp", None),
        P("dp"),
        P("tensor", "dp"),
    )
    return jax.shard_map(
        body,
        mesh=mesh,
        in_specs=placed,
        out_specs=(P("dp", "tensor", None, None, None), P(None, "dp")),
        check_vma=False,
    )
```

profile of v0, /device:TPU:1, one launch (start us, length us, event | category | flops | bytes accessed | tf_op | source)
XLA Modules:
  0.0 194.9 jit_solution(8297206147046076033)
XLA Ops:
  0.6 0.7 slice_bitcast_fusion
  2.2 0.7 add_select_fusion
  3.0 0.7 convert_element_type.79
  3.7 6.4 %all-to-all-start = ((bf16[8,2,1]{1,2,0:T(2,128)(2,1)}), bf16[8,2,1]{1,2,0:T(2,128)(2,1)S(1)}, u32[]{:S(2)}, u32[]{:S(2)}) async-start(bf16[8,2,1]{1,2,0:T(2,128)(2,1)} %convert_element_type.79), calls=%async_computation | async-start | bytes 8192 | tf_op jit(solution)/shard_map/all_to_all | solution.py:41
  10.0 0.7 fusion.16
  10.7 8.8 %pad.2 = bf16[72,512,128]{2,1,0:T(8,128)(2,1)} pad(bf16[70,512,128]{2,1,0:T(8,128)(2,1)} %bitcast.69, bf16[]{:T(256)} %constant.38), padding=0_2x0_0x0_0 | pad | bytes 18612226
  19.5 13.8 %copy.21 = bf16[9,8,512,128]{3,1,2,0:T(8,128)(2,1)} copy(bf16[9,8,512,128]{3,2,1,0:T(8,128)(2,1)} %bitcast.62) | data formatting | bytes 18874368
  33.3 7.8 %gather_fusion = bf16[12,65536]{1,0:T(8,128)(2,1)S(1)} fusion(bf16[70,65536]{1,0:T(8,128)(2,1)} %bitcast.59, s32[1024]{0:T(1024)S(1)} %pad_clamp_fusion.1), kind=kCustom, calls=%fused_computation | custom fusion | bytes 3145776 | tf_op jit(solution)/shard_map/gather | solution.py:31
  41.1 0.7 fusion.4
  41.8 1.9 copy.22
  43.7 5.4 %all-to-all-start.1 = ((bf16[16,2,2,128,128]{4,3,2,1,0:T(8,128)(2,1)}), bf16[16,2,2,128,128]{4,3,2,1,0:T(8,128)(2,1)S(1)}, u32[]{:S(2)}, u32[]{:S(2)}) async-start(bf16[16,2,2,128,128]{4,3,2,1,0:T(8,128)(2,1)} %bitcast.24), calls=%async_computation.1 | async-start | bytes 4194304 | tf_op jit(solution)/shard_map/all_to_all | solution.py:40
  49.5 46.5 %all-to-all-done.1 = bf16[16,2,2,128,128]{4,3,2,1,0:T(8,128)(2,1)S(1)} async-done(((bf16[16,2,2,128,128]{4,3,2,1,0:T(8,128)(2,1)}), bf16[16,2,2,128,128]{4,3,2,1,0:T(8,128)(2,1)S(1)}, u32[]{:S(2)}, u32[]{:S(2)}) %all-to-all-start.1) | async-done | bytes 2097184 | tf_op jit(solution)/shard_map/all_to_all | solution.py:40
  96.0 10.8 %fusion.1 = bf16[70,65536]{1,0:T(8,128)(2,1)} fusion(bf16[70,65536]{1,0:T(8,128)(2,1)} %bitcast.60, pred[70]{0:T(512)(128)(4,1)S(1)} %fusion.12, bf16[2,8,512,128]{3,2,1,0:T(8,128)(2,1)S(1)} %bitcast.70, s32[16]{0:T(128)S(1)} %convert_element_type.72), kind=kOutput, calls=%fused_computation.4 | convolution fusion | flops 155976800 | bytes 20447366 | tf_op jit(solution)/shard_map/dot_general | solution.py:45
  106.8 9.9 %copy.24 = bf16[9,8,512,128]{3,2,1,0:T(8,128)(2,1)} copy(bf16[9,8,512,128]{3,1,2,0:T(8,128)(2,1)} %bitcast.61) | data formatting | bytes 18874368
  116.7 8.4 %slice.29 = bf16[70,512,128]{2,1,0:T(8,128)(2,1)} slice(bf16[72,512,128]{2,1,0:T(8,128)(2,1)} %bitcast.63), slice={[0:70], [0:512], [0:128]} | slice | bytes 18350080
  125.1 9.1 %gather_fusion.1 = bf16[64,2,2,128,128]{4,3,2,1,0:T(8,128)(2,1)} fusion(bf16[70,2,2,128,128]{4,3,2,1,0:T(8,128)(2,1)} %bitcast.64, s32[1024]{0:T(1024)S(1)} %pad_clamp_fusion), kind=kCustom, calls=%fused_computation.1 | custom fusion | bytes 16777472 | tf_op jit(solution)/shard_map/gather | solution.py:57
  134.2 3.8 %fusion.17 = (bf16[8,8,2,1,128,128]{5,4,3,2,1,0:T(8,128)(2,1)S(1)}, bf16[8,8,2,1,128,128]{5,4,3,2,1,0:T(8,128)(2,1)S(1)}) fusion(bf16[8,8,2,2,128,128]{5,4,3,2,1,0:T(8,128)(2,1)} %bitcast.66), kind=kLoop, calls=%fused_computation.41 | loop fusion | bytes 16777216 | tf_op jit(solution)/shard_map/slice | solution.py:58
  138.1 0.6 copy.19
  138.7 1.2 fusion.8
  140.1 2.2 %copy.20 = bf16[8,8,2,1,128,128]{5,4,1,2,0,3:T(8,128)(2,1)} copy(bf16[8,8,2,1,128,128]{5,4,3,2,1,0:T(8,128)(2,1)S(1)} %get-tuple-element.3) | data formatting | bytes 8388608
  142.3 2.9 %fusion.9 = bf16[1,8,16,128]{3,2,1,0:T(8,128)(2,1)S(1)} fusion(bf16[8,2,1024,128]{3,2,1,0:T(8,128)(2,1)} %bitcast.67, f32[8,2,8]{2,1,0:T(2,128)S(1)} %fusion.18, f32[8,2,8,1024]{3,2,1,0:T(8,128)S(1)} %fusion.8), kind=kOutput, calls=%fused_computation.15 | convolution fusion | flops 33965184 | bytes 4751872 | tf_op jit(solution)/shard_map/skgt,sktd->skgd/dot_general | solution.py:75
  145.3 25.4 %all_gather.3 = bf16[64,2048]{1,0:T(8,128)(2,1)S(1)} all-gather(bf16[8,2048]{1,0:T(8,128)(2,1)S(1)} %bitcast.71), channel_id=1, replica_groups=mesh['dp'=8,'tensor'=4] {'dp'}, dimensions={0}, use_global_device_ids=true | all-gather | bytes 294912 | tf_op jit(solution)/shard_map/all_gather | solution.py:82
  170.7 3.0 %fusion.19 = f32[64,1024]{1,0:T(8,128)S(1)} fusion(bf16[64,2048]{1,0:T(8,128)(2,1)S(1)} %all_gather.3, bf16[2048,1024]{1,0:T(8,128)(2,1)} %param.13), kind=kOutput, calls=%fused_computation.43 | convolution fusion | flops 268435456 | bytes 4718592 | tf_op jit(solution)/shard_map/dot_general | solution.py:81
  173.7 21.2 %all-reduce.1 = bf16[64,1024]{1,0:T(8,128)(2,1)} all-reduce(f32[64,1024]{1,0:T(8,128)S(1)} %fusion.19), channel_id=1, replica_groups=mesh['dp'=8,'tensor'=4] {'tensor'}, use_global_device_ids=true, to_apply=%region_5.6 | all-reduce | flops 65536 | bytes 393216 | tf_op jit(solution)/shard_map/psum | solution.py:86
  (21 shorter events, 1.0 us)
Async XLA Ops:
  0.6 138.0 %copy-start = (bf16[8,16,128]{2,1,0:T(8,128)(2,1)S(1)}, bf16[8,16,128]{2,1,0:T(8,128)(2,1)}, u32[]{:S(2)}) copy-start(bf16[8,16,128]{2,1,0:T(8,128)(2,1)} %param.7) | copy-start | bytes 98308
  3.7 40.1 %all-to-all-start = ((bf16[8,2,1]{1,2,0:T(2,128)(2,1)}), bf16[8,2,1]{1,2,0:T(2,128)(2,1)S(1)}, u32[]{:S(2)}, u32[]{:S(2)}) async-start(bf16[8,2,1]{1,2,0:T(2,128)(2,1)} %convert_element_type.79), calls=%async_computation | async-start | bytes 8192 | tf_op jit(solution)/shard_map/all_to_all | solution.py:41
  41.8 7.3 %copy-start.1 = (s32[8,8]{1,0:T(8,128)S(1)}, s32[8,8]{1,0:T(8,128)}, u32[]{:S(2)}) copy-start(s32[8,8]{1,0:T(8,128)} %param.11) | copy-start | bytes 772
  41.8 7.4 %copy-start.2 = (s32[8]{0:T(128)S(1)}, s32[8]{0:T(128)}, u32[]{:S(2)}) copy-start(s32[8]{0:T(128)} %param.12) | copy-start | bytes 100
  43.7 52.3 %all-to-all-start.1 = ((bf16[16,2,2,128,128]{4,3,2,1,0:T(8,128)(2,1)}), bf16[16,2,2,128,128]{4,3,2,1,0:T(8,128)(2,1)S(1)}, u32[]{:S(2)}, u32[]{:S(2)}) async-start(bf16[16,2,2,128,128]{4,3,2,1,0:T(8,128)(2,1)} %bitcast.24), calls=%async_computation.1 | async-start | bytes 4194304 | tf_op jit(solution)/shard_map/all_to_all | solution.py:40
where the time goes:
time: 196 us; the launch traced here: 195 us
  local copies, waits for them, and re-layouts  67.2 us (34%)
  blocking collectives  46.6 us (24%)
  waiting for transfers between devices  46.5 us (24%)
  matrix products  18.6 us (9%)
  starting transfers between devices  11.8 us (6%)
  other arithmetic  2.78 us (1%)
    all_to_all x1, waiting for transfers between devices, body(): lax.all_to_all(outgoing, 'dp', split_axis=0, concat_axis=0, tiled=True)  46.5 us
    unnamed x14, local copies, waits for them, and re-layouts  45.6 us
    all_gather x1, blocking collectives, body(): lax.all_gather(attention, 'dp', axis=0, tiled=True)  25.4 us
    psum x1, blocking collectives, body(): summed = lax.psum(partial_sums, 'tensor')  21.2 us
    dot_general x1, matrix products, body(): jnp.dot(hit_table.astype(jnp.bfloat16), arrived.reshape(holding_rows, -1)...  10.8 us
    gather x1, local copies, waits for them, and re-layouts, body(): gathered = new_pages[block_table]  9.14 us
    gather x1, local copies, waits for them, and re-layouts, body(): picked = flat_pages[move_list[0]]  7.81 us
    all_to_all x1, starting transfers between devices, body(): lax.all_to_all(slot_tags, 'dp', split_axis=0, concat_axis=0, tiled=True)  6.37 us
  transfers between devices with their start and end apart: 2, of which 1 were waited for; matrix products, arithmetic and copies ran while one was open for 17% of the time, Pallas kernels for 0%

commit v1 on v0

--- a/solution.py
+++ b/solution.py
@@ -83,7 +83,14 @@
         out_weight,
         preferred_element_type=jnp.float32,
     )
-    summed = lax.psum(partial_sums, "tensor")
+    n_parts = jax.lax.axis_size("tensor")
+    summed, current_block = (partial_sums, 0)
+    while 1 << current_block < n_parts:
+        then = jax.lax.ppermute(
+            summed, "tensor", perm=[(ix, ix ^ 1 << current_block) for ix in range(n_parts)]
+        )
+        summed = summed + then
+        current_block = current_block + 1
     return (new_pages, summed.astype(jnp.bfloat16))
 
 

time: 196 us -> 193 us (0.985)
  blocking collectives: 46.6 us -> 25.4 us
  starting transfers between devices: 11.8 us -> 20.8 us
  waiting for transfers between devices: 46.5 us -> 53.9 us
    psum x1 -> x0, blocking collectives: 21.2 us -> none  [body(): summed = lax.psum(partial_sums, 'tensor')]
    ppermute x0 -> x2, starting transfers between devices: none -> 9.01 us  [body(): jax.lax.ppermute(summed, 'tensor', perm=[(ix, ix ^ 1 << current_block) fo...]
    ppermute x0 -> x2, waiting for transfers between devices: none -> 7.44 us  [body(): jax.lax.ppermute(summed, 'tensor', perm=[(ix, ix ^ 1 << current_block) fo...]
  transfers between devices with their start and end apart: 2 -> 4, of which waited for: 1 -> 3; matrix products, arithmetic and copies ran while one was open for 17% -> 18% of each run, Pallas kernels for 0% -> 0%
where the time goes in v1:
time: 193 us; the launch traced here: 191 us
  local copies, waits for them, and re-layouts  67.2 us (35%)
  waiting for transfers between devices  53.9 us (28%)
  blocking collectives  25.4 us (13%)
  starting transfers between devices  20.8 us (11%)
  matrix products  18.6 us (10%)
  other arithmetic  3.51 us (2%)
    all_to_all x1, waiting for transfers between devices, body(): lax.all_to_all(outgoing, 'dp', split_axis=0, concat_axis=0, tiled=True)  46.5 us
    unnamed x14, local copies, waits for them, and re-layouts  45.6 us
    all_gather x1, blocking collectives, body(): lax.all_gather(attention, 'dp', axis=0, tiled=True)  25.4 us
    dot_general x1, matrix products, body(): jnp.dot(hit_table.astype(jnp.bfloat16), arrived.reshape(holding_rows, -1)...  10.8 us
    gather x1, local copies, waits for them, and re-layouts, body(): gathered = new_pages[block_table]  9.14 us
    ppermute x2, starting transfers between devices, body(): jax.lax.ppermute(summed, 'tensor', perm=[(ix, ix ^ 1 << current_block) fo...  9.01 us
    gather x1, local copies, waits for them, and re-layouts, body(): picked = flat_pages[move_list[0]]  7.81 us
    ppermute x2, waiting for transfers between devices, body(): jax.lax.ppermute(summed, 'tensor', perm=[(ix, ix ^ 1 << current_block) fo...  7.44 us
  transfers between devices with their start and end apart: 4, of which 3 were waited for; matrix products, arithmetic and copies ran while one was open for 18% of the time, Pallas kernels for 0%

profile of v1, /device:TPU:1, one launch (start us, length us, event | category | flops | bytes accessed | tf_op | source)
XLA Modules:
  0.0 190.9 jit_solution(7469304974899114664)
XLA Ops:
  3.0 0.7 convert_element_type.79
  3.7 6.4 %all-to-all-start = ((bf16[8,2,1]{1,2,0:T(2,128)(2,1)}), bf16[8,2,1]{1,2,0:T(2,128)(2,1)S(1)}, u32[]{:S(2)}, u32[]{:S(2)}) async-start(bf16[8,2,1]{1,2,0:T(2,128)(2,1)} %convert_element_type.79), calls=%async_computation | async-start | bytes 8192 | tf_op jit(solution)/shard_map/all_to_all | solution.py:41
  10.7 8.8 %pad.2 = bf16[72,512,128]{2,1,0:T(8,128)(2,1)} pad(bf16[70,512,128]{2,1,0:T(8,128)(2,1)} %bitcast.69, bf16[]{:T(256)} %constant.38), padding=0_2x0_0x0_0 | pad | bytes 18612226
  19.5 13.8 %copy.21 = bf16[9,8,512,128]{3,1,2,0:T(8,128)(2,1)} copy(bf16[9,8,512,128]{3,2,1,0:T(8,128)(2,1)} %bitcast.62) | data formatting | bytes 18874368
  33.3 7.8 %gather_fusion = bf16[12,65536]{1,0:T(8,128)(2,1)S(1)} fusion(bf16[70,65536]{1,0:T(8,128)(2,1)} %bitcast.59, s32[1024]{0:T(1024)S(1)} %pad_clamp_fusion.1), kind=kCustom, calls=%fused_computation | custom fusion | bytes 3145776 | tf_op jit(solution)/shard_map/gather | solution.py:31
  41.1 0.7 fusion.4
  41.8 1.9 copy.22
  43.7 5.4 %all-to-all-start.1 = ((bf16[16,2,2,128,128]{4,3,2,1,0:T(8,128)(2,1)}), bf16[16,2,2,128,128]{4,3,2,1,0:T(8,128)(2,1)S(1)}, u32[]{:S(2)}, u32[]{:S(2)}) async-start(bf16[16,2,2,128,128]{4,3,2,1,0:T(8,128)(2,1)} %bitcast.24), calls=%async_computation.1 | async-start | bytes 4194304 | tf_op jit(solution)/shard_map/all_to_all | solution.py:40
  49.5 46.5 %all-to-all-done.1 = bf16[16,2,2,128,128]{4,3,2,1,0:T(8,128)(2,1)S(1)} async-done(((bf16[16,2,2,128,128]{4,3,2,1,0:T(8,128)(2,1)}), bf16[16,2,2,128,128]{4,3,2,1,0:T(8,128)(2,1)S(1)}, u32[]{:S(2)}, u32[]{:S(2)}) %all-to-all-start.1) | async-done | bytes 2097184 | tf_op jit(solution)/shard_map/all_to_all | solution.py:40
  96.0 10.8 %fusion.1 = bf16[70,65536]{1,0:T(8,128)(2,1)} fusion(bf16[70,65536]{1,0:T(8,128)(2,1)} %bitcast.60, pred[70]{0:T(512)(128)(4,1)S(1)} %fusion.12, bf16[2,8,512,128]{3,2,1,0:T(8,128)(2,1)S(1)} %bitcast.70, s32[16]{0:T(128)S(1)} %convert_element_type.72), kind=kOutput, calls=%fused_computation.4 | convolution fusion | flops 155976800 | bytes 20447366 | tf_op jit(solution)/shard_map/dot_general | solution.py:45
  106.8 9.9 %copy.24 = bf16[9,8,512,128]{3,2,1,0:T(8,128)(2,1)} copy(bf16[9,8,512,128]{3,1,2,0:T(8,128)(2,1)} %bitcast.61) | data formatting | bytes 18874368
  116.7 8.4 %slice.29 = bf16[70,512,128]{2,1,0:T(8,128)(2,1)} slice(bf16[72,512,128]{2,1,0:T(8,128)(2,1)} %bitcast.63), slice={[0:70], [0:512], [0:128]} | slice | bytes 18350080
  125.1 9.1 %gather_fusion.1 = bf16[64,2,2,128,128]{4,3,2,1,0:T(8,128)(2,1)} fusion(bf16[70,2,2,128,128]{4,3,2,1,0:T(8,128)(2,1)} %bitcast.64, s32[1024]{0:T(1024)S(1)} %pad_clamp_fusion), kind=kCustom, calls=%fused_computation.1 | custom fusion | bytes 16777472 | tf_op jit(solution)/shard_map/gather | solution.py:57
  134.2 3.8 %fusion.17 = (bf16[8,8,2,1,128,128]{5,4,3,2,1,0:T(8,128)(2,1)S(1)}, bf16[8,8,2,1,128,128]{5,4,3,2,1,0:T(8,128)(2,1)S(1)}) fusion(bf16[8,8,2,2,128,128]{5,4,3,2,1,0:T(8,128)(2,1)} %bitcast.66), kind=kLoop, calls=%fused_computation.42 | loop fusion | bytes 16777216 | tf_op jit(solution)/shard_map/slice | solution.py:58
  138.7 1.2 fusion.8
  140.1 2.2 %copy.20 = bf16[8,8,2,1,128,128]{5,4,1,2,0,3:T(8,128)(2,1)} copy(bf16[8,8,2,1,128,128]{5,4,3,2,1,0:T(8,128)(2,1)S(1)} %get-tuple-element.3) | data formatting | bytes 8388608
  142.3 2.9 %fusion.9 = bf16[1,8,16,128]{3,2,1,0:T(8,128)(2,1)S(1)} fusion(bf16[8,2,1024,128]{3,2,1,0:T(8,128)(2,1)} %bitcast.67, f32[8,2,8]{2,1,0:T(2,128)S(1)} %fusion.18, f32[8,2,8,1024]{3,2,1,0:T(8,128)S(1)} %fusion.8), kind=kOutput, calls=%fused_computation.15 | convolution fusion | flops 33965184 | bytes 4751872 | tf_op jit(solution)/shard_map/skgt,sktd->skgd/dot_general | solution.py:75
  145.3 25.4 %all_gather.3 = bf16[64,2048]{1,0:T(8,128)(2,1)S(1)} all-gather(bf16[8,2048]{1,0:T(8,128)(2,1)S(1)} %bitcast.71), channel_id=1, replica_groups=mesh['dp'=8,'tensor'=4] {'dp'}, dimensions={0}, use_global_device_ids=true | all-gather | bytes 294912 | tf_op jit(solution)/shard_map/all_gather | solution.py:82
  170.7 3.0 %fusion.19 = f32[64,1024]{1,0:T(8,128)S(1)} fusion(bf16[64,2048]{1,0:T(8,128)(2,1)S(1)} %all_gather.3, bf16[2048,1024]{1,0:T(8,128)(2,1)} %param.13), kind=kOutput, calls=%fused_computation.44 | convolution fusion | flops 268435456 | bytes 4718592 | tf_op jit(solution)/shard_map/dot_general | solution.py:81
  173.7 7.7 %collective-permute-start = (f32[64,1024]{1,0:T(8,128)S(1)}, f32[64,1024]{1,0:T(8,128)S(1)}, u32[]{:S(2)}, u32[]{:S(2)}) collective-permute-start(f32[64,1024]{1,0:T(8,128)S(1)} %fusion.19), channel_id=1, source_target_pairs={{0,1},{1,0},{2,3},{3,2},{4,5},{5,4},{6,7},{7,6},{8,9},{9,8},{10,11... | collective-permute-start | bytes 786440 | tf_op jit(solution)/shard_map/ppermute | solution.py:89
  181.4 1.2 collective-permute-done
  182.7 1.3 collective-permute-start.1
  183.9 6.3 %collective-permute-done.1 = f32[64,1024]{1,0:T(8,128)S(1)} collective-permute-done((f32[64,1024]{1,0:T(8,128)S(1)}, f32[64,1024]{1,0:T(8,128)S(1)}, u32[]{:S(2)}, u32[]{:S(2)}) %collective-permute-start.1) | collective-permute-done | bytes 262176 | tf_op jit(solution)/shard_map/ppermute | solution.py:89
  190.2 0.7 add_convert_fusion
  (26 shorter events, 3.6 us)
Async XLA Ops:
  0.6 138.0 %copy-start = (bf16[8,16,128]{2,1,0:T(8,128)(2,1)S(1)}, bf16[8,16,128]{2,1,0:T(8,128)(2,1)}, u32[]{:S(2)}) copy-start(bf16[8,16,128]{2,1,0:T(8,128)(2,1)} %param.7) | copy-start | bytes 98308
  3.7 40.1 %all-to-all-start = ((bf16[8,2,1]{1,2,0:T(2,128)(2,1)}), bf16[8,2,1]{1,2,0:T(2,128)(2,1)S(1)}, u32[]{:S(2)}, u32[]{:S(2)}) async-start(bf16[8,2,1]{1,2,0:T(2,128)(2,1)} %convert_element_type.79), calls=%async_computation | async-start | bytes 8192 | tf_op jit(solution)/shard_map/all_to_all | solution.py:41
  41.8 7.3 %copy-start.1 = (s32[8,8]{1,0:T(8,128)S(1)}, s32[8,8]{1,0:T(8,128)}, u32[]{:S(2)}) copy-start(s32[8,8]{1,0:T(8,128)} %param.11) | copy-start | bytes 772
  41.8 7.4 %copy-start.2 = (s32[8]{0:T(128)S(1)}, s32[8]{0:T(128)}, u32[]{:S(2)}) copy-start(s32[8]{0:T(128)} %param.12) | copy-start | bytes 100
  43.7 52.3 %all-to-all-start.1 = ((bf16[16,2,2,128,128]{4,3,2,1,0:T(8,128)(2,1)}), bf16[16,2,2,128,128]{4,3,2,1,0:T(8,128)(2,1)S(1)}, u32[]{:S(2)}, u32[]{:S(2)}) async-start(bf16[16,2,2,128,128]{4,3,2,1,0:T(8,128)(2,1)} %bitcast.24), calls=%async_computation.1 | async-start | bytes 4194304 | tf_op jit(solution)/shard_map/all_to_all | solution.py:40
  173.7 8.9 %collective-permute-start = (f32[64,1024]{1,0:T(8,128)S(1)}, f32[64,1024]{1,0:T(8,128)S(1)}, u32[]{:S(2)}, u32[]{:S(2)}) collective-permute-start(f32[64,1024]{1,0:T(8,128)S(1)} %fusion.19), channel_id=1, source_target_pairs={{0,1},{1,0},{2,3},{3,2},{4,5},{5,4},{6,7},{7,6},{8,9},{9,8},{10,11... | collective-permute-start | bytes 786440 | tf_op jit(solution)/shard_map/ppermute | solution.py:89
  182.7 7.6 %collective-permute-start.1 = (f32[64,1024]{1,0:T(8,128)S(1)}, f32[64,1024]{1,0:T(8,128)S(1)}, u32[]{:S(2)}, u32[]{:S(2)}) collective-permute-start(f32[64,1024]{1,0:T(8,128)S(1)} %add.55), channel_id=1, source_target_pairs={{0,2},{1,3},{2,0},{3,1},{4,6},{5,7},{6,4},{7,5},{8,10},{9,11},{10,... | collective-permute-start | bytes 786440 | tf_op jit(solution)/shard_map/ppermute | solution.py:89
